TPU v7x, 128 devices: a whole 4x4x4 slice. The times are simulated.
128 devices in a mesh: brick: 8 (over y, core), grp: 16 (over x, z).
Axes of the slice: x: 4, y: 4, z: 4, core: 2. Of those that a mesh axis runs over, the one named last changes fastest.
Arguments:
- source: float32 [16, 8, 2, 32, 1024], P('grp', 'brick'), may hold values from -21 to 21
- uptake: float32 [16, 8, 2, 32, 1024], P('grp', 'brick'), may hold values from 0.00015 to 0.006
- conductance: float32 [16, 8, 6, 2, 32, 1024], P('grp', 'brick'), may hold values from 0 to 3, as said below
- occupancy: int32 [16, 2, 8], replicated, may hold values from 0 to 1, as said below
- assignment: int32 [8], replicated, may hold values from 0 to 7, as said below
Outputs:
- solution_field: float32 [16, 8, 2, 32, 1024], P('grp', 'brick')
- residual: float32 [16, 8, 2, 32, 1024], P('grp', 'brick')
Inputs may be any that keep to these rules, and one draw needn't show every extreme that they name: `occupancy`: 1 marks an occupied brick; in every draw one patch of some slab has all its bricks occupied. `assignment`: each patch is held by exactly one index of brick. `conductance`: equal at both ends of a bond: the value toward +x at a cell is the value toward -x at its +x neighbour, likewise for y and z, the lattice being read cyclically; values toward +z and -z are 0.3 or more.
All inputs are finite; a program needn't handle non-finite values.
Results may differ from a plain program's by a relative error of at most 0.0003.
Values sent between devices are 32-bit elements; how exact they have to be, the bound alone decides.
A program may use at most 128 MiB of HBM per device.

v0:
```python
import jax
import jax.numpy as jnp
from jax import lax
from jax.sharding import PartitionSpec as P

BS = 32
PATCH_X = 1
PATCH_Y = 2
ITERS = 3
OMEGA = 0.6


def extended_2(block, sides, width):
    for axis, dim in sides:
        count = lax.axis_size(axis)
        forward = [(i, i + 1) for i in range(count - 1)]
        backward = [(target, source) for source, target in forward]
        low = lax.ppermute(
            lax.slice_in_dim(block, block.shape[dim] - width, None, axis=dim), axis, forward
        )
        high = lax.ppermute(lax.slice_in_dim(block, 0, width, axis=dim), axis, backward)
        block = jnp.concatenate([low, block, high], axis=dim)
    return block


def assemble(coarse_diag, couplings, strides):
    extent = coarse_diag.shape[0]
    matrix = jnp.diag(coarse_diag)
    for coupling, stride in zip(couplings, strides):
        banded = coupling[: extent - stride]
        matrix = matrix - jnp.diag(banded, stride) - jnp.diag(banded, -stride)
    return matrix


def pad_rows(block, capacity):
    return jnp.pad(block, ((0, capacity - block.shape[0]), (0, 0)))


def on_device(source, uptake, conductance, occupancy, assignment):
    face_size = BS * BS
    capacity = max(PATCH_X, PATCH_Y)
    slot_count = PATCH_X * PATCH_Y
    slab_index = lax.axis_index("grp")
    brick_index = lax.axis_index("brick")
    brick_count = lax.axis_size("brick")
    across = brick_count // 2
    peer_ids = jnp.arange(brick_count, dtype=jnp.int32)
    patch_index = assignment[brick_index]
    patch_row = patch_index // across
    patch_column = patch_index % across

    def owner_of(row_shift, column_shift):
        row_target = patch_row + row_shift
        column_target = patch_column + column_shift
        inside = (
            (row_target >= 0) & (row_target < 2) & (column_target >= 0) & (column_target < across)
        )
        holder = jnp.sum(jnp.where(assignment == row_target * across + column_target, peer_ids, 0))
        return jnp.where(inside, holder, -1)

    wanted = jnp.stack([owner_of(1, 0), owner_of(-1, 0), owner_of(0, 1), owner_of(0, -1)])
    padded = jnp.pad(occupancy, 1)
    window = lax.dynamic_slice(
        padded,
        (slab_index, patch_row * PATCH_X, patch_column * PATCH_Y),
        (3, PATCH_X + 2, PATCH_Y + 2),
    ).astype(jnp.float32)
    centre = window[1, 1:-1, 1:-1].reshape(slot_count)
    toward = [
        window[1, 2:, 1:-1],
        window[1, :-2, 1:-1],
        window[1, 1:-1, 2:],
        window[1, 1:-1, :-2],
        window[2, 1:-1, 1:-1],
        window[0, 1:-1, 1:-1],
    ]
    first_axis = lax.broadcasted_iota(jnp.int32, (1, BS, face_size), 1)
    flat_axis = lax.broadcasted_iota(jnp.int32, (1, BS, face_size), 2)
    second_axis = flat_axis // BS
    third_axis = flat_axis % BS
    cube_third = lax.broadcasted_iota(jnp.int32, (1, BS, BS, BS), 3)
    borders = [
        first_axis == BS - 1,
        first_axis == 0,
        second_axis == BS - 1,
        second_axis == 0,
        third_axis == BS - 1,
        third_axis == 0,
    ]
    bonds = conductance[0, 0]
    live_here = centre[:, None, None]
    effective = []
    for direction in range(6):
        neighbour_live = toward[direction].reshape(slot_count)[:, None, None]
        active = jnp.where(borders[direction], live_here * neighbour_live, live_here)
        effective.append(bonds[direction] * active)
    absorb = uptake[0, 0]
    diagonal = absorb
    for direction in range(6):
        diagonal = diagonal + effective[direction]

    def apply_operator(field):
        lower_x = field[:, 0, :]
        upper_x = field[:, BS - 1, :]
        lower_y = field[:, :, :BS].reshape(slot_count, face_size)
        upper_y = field[:, :, face_size - BS :].reshape(slot_count, face_size)
        cube = field.reshape(slot_count, BS, BS, BS)
        lower_z = cube[:, :, :, 0].reshape(slot_count, face_size)
        upper_z = cube[:, :, :, BS - 1].reshape(slot_count, face_size)
        grid_lower_x = lower_x.reshape(PATCH_X, PATCH_Y, face_size)
        grid_upper_x = upper_x.reshape(PATCH_X, PATCH_Y, face_size)
        grid_lower_y = lower_y.reshape(PATCH_X, PATCH_Y, face_size)
        grid_upper_y = upper_y.reshape(PATCH_X, PATCH_Y, face_size)
        outgoing_sides = jnp.stack(
            [
                pad_rows(grid_lower_x[0], capacity),
                pad_rows(grid_upper_x[PATCH_X - 1], capacity),
                pad_rows(grid_lower_y[:, 0], capacity),
                pad_rows(grid_upper_y[:, PATCH_Y - 1], capacity),
            ]
        )
        portion = lax.all_gather(outgoing_sides[None], "brick", axis=0, tiled=True)
        sources = jnp.arange(portion.shape[0], dtype=jnp.int32)
        matches = sources[:, None] == wanted[None, :]
        remote = jnp.zeros((4, capacity, face_size), jnp.float32) + jnp.sum(
            jnp.where(matches[:, :, None, None], portion, 0.0), axis=0
        )
        stacked = jnp.stack([lower_z, upper_z])
        extended = extended_2(stacked, (("grp", 0),), 1)
        from_below = extended[0].reshape(slot_count, BS, BS, 1)
        from_above = extended[3].reshape(slot_count, BS, BS, 1)
        beyond_xplus = jnp.concatenate(
            [grid_lower_x[1:], remote[0, :PATCH_Y][None]], axis=0
        ).reshape(slot_count, face_size)
        beyond_xminus = jnp.concatenate(
            [remote[1, :PATCH_Y][None], grid_upper_x[:-1]], axis=0
        ).reshape(slot_count, face_size)
        beyond_yplus = jnp.concatenate(
            [grid_lower_y[:, 1:], remote[2, :PATCH_X][:, None]], axis=1
        ).reshape(slot_count, BS, BS)
        beyond_yminus = jnp.concatenate(
            [remote[3, :PATCH_X][:, None], grid_upper_y[:, :-1]], axis=1
        ).reshape(slot_count, BS, BS)
        upper_neighbour = jnp.where(
            cube_third == BS - 1, from_above, jnp.roll(cube, -1, axis=3)
        ).reshape(slot_count, BS, face_size)
        lower_neighbour = jnp.where(cube_third == 0, from_below, jnp.roll(cube, 1, axis=3)).reshape(
            slot_count, BS, face_size
        )
        total = diagonal * field
        total = total - effective[0] * jnp.concatenate(
            [field[:, 1:, :], beyond_xplus[:, None, :]], axis=1
        )
        total = total - effective[1] * jnp.concatenate(
            [beyond_xminus[:, None, :], field[:, :-1, :]], axis=1
        )
        total = total - effective[2] * jnp.concatenate([field[:, :, BS:], beyond_yplus], axis=2)
        total = total - effective[3] * jnp.concatenate(
            [beyond_yminus, field[:, :, : face_size - BS]], axis=2
        )
        total = total - effective[4] * upper_neighbour
        total = total - effective[5] * lower_neighbour
        return total

    slot_ids = jnp.arange(slot_count)
    brick_first = slot_ids // PATCH_Y
    brick_second = slot_ids % PATCH_Y
    inside = [
        (brick_first < PATCH_X - 1).astype(jnp.float32),
        (brick_first > 0).astype(jnp.float32),
        (brick_second < PATCH_Y - 1).astype(jnp.float32),
        (brick_second > 0).astype(jnp.float32),
    ]
    face_sums = [
        jnp.sum(effective[0][:, BS - 1, :], axis=1),
        jnp.sum(effective[1][:, 0, :], axis=1),
        jnp.sum(effective[2][:, :, face_size - BS :], axis=(1, 2)),
        jnp.sum(effective[3][:, :, :BS], axis=(1, 2)),
        jnp.sum(effective[4].reshape(slot_count, BS, BS, BS)[:, :, :, BS - 1], axis=(1, 2)),
        jnp.sum(effective[5].reshape(slot_count, BS, BS, BS)[:, :, :, 0], axis=(1, 2)),
    ]
    coarse_diag = jnp.sum(absorb, axis=(1, 2))
    for direction in range(4):
        coarse_diag = coarse_diag + face_sums[direction] * inside[direction]
    coarse_diag = coarse_diag + face_sums[4] + face_sums[5]
    grp_count = lax.axis_size("grp")
    grp_ids = jnp.arange(grp_count, dtype=jnp.int32)

    def butterfly(values, axes):
        for axis in axes:
            count = lax.axis_size(axis)
            if count & count - 1:
                values = lax.psum(values, axis)
                continue
            stride = 1
            while stride < count:
                pairs = [(i, i ^ stride) for i in range(count)]
                values = values + lax.ppermute(values, axis, pairs)
                stride *= 2
        return values

    def slab_slot(values):
        here = (grp_ids == slab_index).astype(jnp.float32)
        return here[:, None, None] * values[None]

    forcing = source[0, 0] * live_here
    record = jnp.stack(
        [
            coarse_diag,
            face_sums[0] * inside[0],
            face_sums[2] * inside[2],
            face_sums[4],
            jnp.sum(forcing, axis=(1, 2)),
        ]
    )
    gathered = butterfly(slab_slot(record), ("grp",))
    columns = jnp.transpose(gathered, (1, 0, 2)).reshape(5, -1)
    matrix = assemble(columns[0], (columns[1], columns[2], columns[3]), (PATCH_Y, 1, slot_count))
    factor = jnp.linalg.cholesky(matrix)

    def coarse_solve(terms):
        middle = lax.linalg.triangular_solve(factor, terms[:, None], left_side=True, lower=True)
        result = lax.linalg.triangular_solve(
            factor, middle, left_side=True, lower=True, transpose_a=True
        )
        return lax.dynamic_slice_in_dim(result[:, 0], slab_index * slot_count, slot_count)

    def precondition(residual_field, terms):
        smoothed = OMEGA * residual_field / diagonal
        smoothed = smoothed + OMEGA * (residual_field - apply_operator(smoothed)) / diagonal
        return smoothed + coarse_solve(terms)[:, None, None]

    brick_here = (peer_ids == brick_index).astype(jnp.float32)

    def dot_and_sums(product, field):
        sums = slab_slot(jnp.sum(field, axis=(1, 2))[None])[:, 0]
        spread = brick_here[:, None, None] * sums[None]
        packed = jnp.concatenate([jnp.sum(product)[None], spread.reshape(-1)])
        total = butterfly(packed, ("brick", "grp"))
        mine = lax.dynamic_index_in_dim(
            total[1:].reshape(brick_count, -1), brick_index, keepdims=False
        )
        return (total[0], mine)

    def global_sum(values):
        return butterfly(jnp.sum(values)[None], ("brick", "grp"))[0]

    terms = columns[4]
    solution_field = jnp.zeros_like(forcing)
    residual = forcing
    search = precondition(residual, terms)
    energy = global_sum(residual * search)
    for iteration in range(ITERS):
        mapped = apply_operator(search)
        curvature, mapped_terms = dot_and_sums(search * mapped, mapped)
        step_size = energy / curvature
        solution_field = solution_field + step_size * search
        residual = residual - step_size * mapped
        if iteration + 1 < ITERS:
            terms = terms - step_size * mapped_terms
            smoothed = precondition(residual, terms)
            renewed = global_sum(residual * smoothed)
            search = smoothed + renewed / energy * search
            energy = renewed
    return (solution_field[None, None], residual[None, None])


def solution(mesh):
    return jax.shard_map(
        on_device,
        mesh=mesh,
        in_specs=(
            P("grp", "brick", None, None, None),
            P("grp", "brick", None, None, None),
            P("grp", "brick", None, None, None, None),
            P(),
            P(),
        ),
        out_specs=(P("grp", "brick", None, None, None), P("grp", "brick", None, None, None)),
        check_vma=False,
    )
```

profile of v0, /device:TPU:0, one launch (start us, length us, event | category | flops | bytes accessed | tf_op | source)
XLA Modules:
  0.0 795.7 jit_solution(16637626487733563843)
XLA Ops:
  31.3 5.5 multiply_divide_fusion.2
  62.5 13.4 %all-gather = f32[32,2,1024]{2,1,0:T(2,128)S(1)} all-gather(f32[4,2,1024]{2,1,0:T(2,128)S(1)} %copy.421), channel_id=2, replica_groups=mesh['brick'=8,'grp'=16] {'brick'}, dimensions={0}, use_global_device_ids=true | all-gather | bytes 294912 | tf_op jit(solution)/shard_map/all_gather | solution.py:122
  84.2 5.6 collective-permute-start.3
  92.7 3.5 collective-permute-start.4
  102.1 3.0 collective-permute-start.5
  112.6 2.9 cholesky.19
  121.3 8.5 %fusion.46 = (f32[2,32,32,32]{3,2,1,0:T(8,128)S(1)}, f32[2,32,32,32]{3,2,1,0:T(8,128)}, f32[2,32,32,32]{3,2,1,0:T(8,128)}) fusion(f32[2,32,32,32]{3,2,1,0:T(8,128)} %get-tuple-element.73, f32[2,32,32,32]{3,2,1,0:T(8,128)} %copy-done.15, f32[2,32,32,32]{3,2,1,0:T(8,128)} %copy-done.14, f32[2,32,32,32]{3,2,1,0:T(8,128)} %concatenate.668, ...), kind=kLoop, calls=%fused_computation.88 | loop fusion | flops 2293760 | bytes 4538480 | tf_op jit(solution)/shard_map/add | solution.py:231
  152.9 12.8 %all-gather.1 = f32[32,2,1024]{2,1,0:T(2,128)S(1)} all-gather(f32[4,2,1024]{2,1,0:T(2,128)S(1)} %copy.424), channel_id=3, replica_groups=mesh['brick'=8,'grp'=16] {'brick'}, dimensions={0}, use_global_device_ids=true | all-gather | bytes 294912 | tf_op jit(solution)/shard_map/all_gather | solution.py:122
  181.4 3.0 pad_maximum_fusion.2
  206.9 3.8 multiply_reduce_fusion.4
  222.3 3.2 collective-permute-done.17
  229.7 3.5 collective-permute-start.19
  235.4 4.4 collective-permute-start.20
  259.0 3.3 collective-permute-start.8
  270.3 3.7 collective-permute-done.10
  278.8 3.7 collective-permute-start.12
  296.8 13.2 %all-gather.2 = f32[32,2,1024]{2,1,0:T(2,128)S(1)} all-gather(f32[4,2,1024]{2,1,0:T(2,128)S(1)} %copy.430), channel_id=4, replica_groups=mesh['brick'=8,'grp'=16] {'brick'}, dimensions={0}, use_global_device_ids=true | all-gather | bytes 294912 | tf_op jit(solution)/shard_map/all_gather | solution.py:122
  315.7 6.9 multiply_divide_fusion.1
  338.7 3.0 pad_maximum_fusion.4
  372.2 3.8 multiply_reduce_fusion.3
  386.1 3.3 collective-permute-start.26
  391.8 4.0 collective-permute-start.27
  396.5 3.8 collective-permute-start.28
  402.3 5.7 collective-permute-start.29
  408.8 4.9 collective-permute-start.30
  417.2 13.0 %all-gather.3 = f32[32,2,1024]{2,1,0:T(2,128)S(1)} all-gather(f32[4,2,1024]{2,1,0:T(2,128)S(1)} %copy.435), channel_id=5, replica_groups=mesh['brick'=8,'grp'=16] {'brick'}, dimensions={0}, use_global_device_ids=true | all-gather | bytes 294912 | tf_op jit(solution)/shard_map/all_gather | solution.py:122
  434.1 6.3 multiply_add_fusion.1
  467.3 3.4 multiply_reduce_fusion.2
  479.1 3.2 collective-permute-done.35
  486.5 4.1 collective-permute-start.37
  492.2 5.5 collective-permute-start.38
  499.9 3.6 collective-permute-start.39
  517.4 13.1 %all-gather.4 = f32[32,2,1024]{2,1,0:T(2,128)S(1)} all-gather(f32[4,2,1024]{2,1,0:T(2,128)S(1)} %copy.440), channel_id=6, replica_groups=mesh['brick'=8,'grp'=16] {'brick'}, dimensions={0}, use_global_device_ids=true | all-gather | bytes 294912 | tf_op jit(solution)/shard_map/all_gather | solution.py:122
  535.4 6.6 multiply_divide_fusion
  556.8 3.1 pad_maximum_fusion.8
  589.0 3.9 multiply_reduce_fusion.1
  603.1 3.3 collective-permute-start.44
  608.9 4.0 collective-permute-start.45
  613.9 3.0 collective-permute-start.46
  619.7 4.9 collective-permute-start.47
  625.6 4.0 collective-permute-start.48
  641.0 13.2 %all-gather.5 = f32[32,2,1024]{2,1,0:T(2,128)S(1)} all-gather(f32[4,2,1024]{2,1,0:T(2,128)S(1)} %copy.445), channel_id=7, replica_groups=mesh['brick'=8,'grp'=16] {'brick'}, dimensions={0}, use_global_device_ids=true | all-gather | bytes 294912 | tf_op jit(solution)/shard_map/all_gather | solution.py:122
  659.3 9.3 %multiply_add_fusion = f32[2,32,32,32]{3,2,1,0:T(8,128)S(1)} fusion(f32[2,32,32,32]{3,2,1,0:T(8,128)} %copy-done.16, f32[2,32,32,32]{3,2,1,0:T(8,128)} %get-tuple-element.73, f32[2,32,32,32]{3,2,1,0:T(8,128)} %copy-done.15, f32[2,32,32,32]{3,2,1,0:T(8,128)} %copy-done.14, f32[2,32,32,32]{3,2,1,0:T(8,128)} %concatenate.784, ...), kind=kLoop, calls=%fused_computation.76 | loop fusion | flops 3735552 | bytes 5865592 | tf_op jit(solution)/shard_map/add | solution.py:263
  706.1 3.2 collective-permute-done.53
  713.5 3.8 collective-permute-start.55
  740.0 3.9 fusion.96
  751.7 2.8 collective-permute-start.57
  788.8 5.9 fusion.148
  (954 shorter events, 510.6 us)
Async XLA Ops:
  40.5 42.8 %collective-permute-start.2 = (f32[16,5,2]{2,0,1:T(8,128)}, f32[16,5,2]{2,0,1:T(8,128)}, u32[]{:S(2)}, u32[]{:S(2)}) collective-permute-start(f32[16,5,2]{2,0,1:T(8,128)} %broadcast_multiply_fusion.3), channel_id=1, source_target_pairs={{0,1},{1,0},{2,3},{3,2},{4,5},{5,4},{6,7},{7,6},{8,9},{9,8},{10,11... | collective-permute-start | bytes 1928 | tf_op jit(solution)/shard_map/ppermute | solution.py:198
  46.3 74.2 %collective-permute-start.1 = (f32[1,2,1024]{2,1,0:T(2,128)}, f32[1,2,1024]{2,1,0:T(2,128)}, u32[]{:S(2)}, u32[]{:S(2)}) collective-permute-start(f32[1,2,1024]{2,1,0:T(2,128)} %stack_reshape_squeeze.37), channel_id=1, source_target_pairs={{0,1},{1,2},{2,3},{3,4},{4,5},{5,6},{6,7},{7,8},{8,9},{9,10},{10,1... | collective-permute-start | bytes 24584 | tf_op jit(solution)/shard_map/ppermute | solution.py:18
  50.3 69.5 %collective-permute-start = (f32[1,2,1024]{2,1,0:T(2,128)}, f32[1,2,1024]{2,1,0:T(2,128)}, u32[]{:S(2)}, u32[]{:S(2)}) collective-permute-start(f32[1,2,1024]{2,1,0:T(2,128)} %stack_reshape_squeeze.36), channel_id=1, source_target_pairs={{1,0},{2,1},{3,2},{4,3},{5,4},{6,5},{7,6},{8,7},{9,8},{10,9},{11,1... | collective-permute-start | bytes 24584 | tf_op jit(solution)/shard_map/ppermute | solution.py:21
  84.2 7.6 collective-permute-start.3
  92.7 9.4 %collective-permute-start.4 = (f32[16,5,2]{2,0,1:T(8,128)S(1)}, f32[16,5,2]{2,0,1:T(8,128)S(1)}, u32[]{:S(2)}, u32[]{:S(2)}) collective-permute-start(f32[16,5,2]{2,0,1:T(8,128)S(1)} %fusion.258), channel_id=1, source_target_pairs={{0,4},{1,5},{2,6},{3,7},{4,0},{5,1},{6,2},{7,3},{8,12},{9,13},{10,... | collective-permute-start | bytes 1928 | tf_op jit(solution)/shard_map/ppermute | solution.py:198
  102.1 9.6 %collective-permute-start.5 = (f32[16,5,2]{2,0,1:T(8,128)S(1)}, f32[16,5,2]{2,0,1:T(8,128)S(1)}, u32[]{:S(2)}, u32[]{:S(2)}) collective-permute-start(f32[16,5,2]{2,0,1:T(8,128)S(1)} %add.671), channel_id=1, source_target_pairs={{0,8},{1,9},{2,10},{3,11},{4,12},{5,13},{6,14},{7,15},{8,0},{9,1},... | collective-permute-start | bytes 1928 | tf_op jit(solution)/shard_map/ppermute | solution.py:198
  176.7 18.5 %collective-permute-start.14 = (f32[1,2,1024]{2,1,0:T(2,128)}, f32[1,2,1024]{2,1,0:T(2,128)}, u32[]{:S(2)}, u32[]{:S(2)}) collective-permute-start(f32[1,2,1024]{2,1,0:T(2,128)} %stack_reshape_squeeze.39), channel_id=1, source_target_pairs={{0,1},{1,2},{2,3},{3,4},{4,5},{5,6},{6,7},{7,8},{8,9},{9,10},{10,1... | collective-permute-start | bytes 24584 | tf_op jit(solution)/shard_map/ppermute | solution.py:18
  178.6 22.5 %collective-permute-start.13 = (f32[1,2,1024]{2,1,0:T(2,128)}, f32[1,2,1024]{2,1,0:T(2,128)}, u32[]{:S(2)}, u32[]{:S(2)}) collective-permute-start(f32[1,2,1024]{2,1,0:T(2,128)} %stack_reshape_squeeze.38), channel_id=1, source_target_pairs={{1,0},{2,1},{3,2},{4,3},{5,4},{6,5},{7,6},{8,7},{9,8},{10,9},{11,1... | collective-permute-start | bytes 24584 | tf_op jit(solution)/shard_map/ppermute | solution.py:21
  220.4 5.1 collective-permute-start.17
  225.5 4.2 collective-permute-start.18
  229.7 5.1 collective-permute-start.19
  235.4 16.3 %collective-permute-start.20 = (f32[257]{0:T(512)}, f32[257]{0:T(512)}, u32[]{:S(2)}, u32[]{:S(2)}) collective-permute-start(f32[257]{0:T(512)} %add.700), channel_id=1, source_target_pairs={{0,4},{1,5},{2,6},{3,7},{4,0},{5,1},{6,2},{7,3},{8,12},{9,13},{10,... | collective-permute-start | bytes 3092 | tf_op jit(solution)/shard_map/ppermute | solution.py:198
  247.0 6.6 collective-permute-start.6
  252.4 32.1 %collective-permute-start.21 = (f32[257]{0:T(512)S(1)}, f32[257]{0:T(512)S(1)}, u32[]{:S(2)}, u32[]{:S(2)}) collective-permute-start(f32[257]{0:T(512)S(1)} %add.701), channel_id=1, source_target_pairs={{0,8},{1,9},{2,10},{3,11},{4,12},{5,13},{6,14},{7,15},{8,0},{9,1},... | collective-permute-start | bytes 3092 | tf_op jit(solution)/shard_map/ppermute | solution.py:198
  259.0 5.1 collective-permute-start.8
  268.9 5.1 collective-permute-start.10
  278.8 5.1 collective-permute-start.12
  332.4 28.0 %collective-permute-start.23 = (f32[1,2,1024]{2,1,0:T(2,128)}, f32[1,2,1024]{2,1,0:T(2,128)}, u32[]{:S(2)}, u32[]{:S(2)}) collective-permute-start(f32[1,2,1024]{2,1,0:T(2,128)} %stack_reshape_squeeze.41), channel_id=1, source_target_pairs={{0,1},{1,2},{2,3},{3,4},{4,5},{5,6},{6,7},{7,8},{8,9},{9,10},{10,1... | collective-permute-start | bytes 24584 | tf_op jit(solution)/shard_map/ppermute | solution.py:18
  334.9 31.4 %collective-permute-start.22 = (f32[1,2,1024]{2,1,0:T(2,128)}, f32[1,2,1024]{2,1,0:T(2,128)}, u32[]{:S(2)}, u32[]{:S(2)}) collective-permute-start(f32[1,2,1024]{2,1,0:T(2,128)} %stack_reshape_squeeze.40), channel_id=1, source_target_pairs={{1,0},{2,1},{3,2},{4,3},{5,4},{6,5},{7,6},{8,7},{9,8},{10,9},{11,1... | collective-permute-start | bytes 24584 | tf_op jit(solution)/shard_map/ppermute | solution.py:21
  375.9 4.7 collective-permute-start.24
  386.1 5.1 collective-permute-start.26
  391.8 4.1 collective-permute-start.27
  396.5 5.1 collective-permute-start.28
  402.3 5.9 collective-permute-start.29
  408.8 5.1 collective-permute-start.30
  444.3 13.6 %collective-permute-start.32 = (f32[1,2,1024]{2,1,0:T(2,128)S(1)}, f32[1,2,1024]{2,1,0:T(2,128)S(1)}, u32[]{:S(2)}, u32[]{:S(2)}) collective-permute-start(f32[1,2,1024]{2,1,0:T(2,128)S(1)} %stack_reshape_squeeze.43), channel_id=1, source_target_pairs={{0,1},{1,2},{2,3},{3,4},{4,5},{5,6},{6,7},{7,8},{8,9},{9,10},{10,1... | collective-permute-start | bytes 24584 | tf_op jit(solution)/shard_map/ppermute | solution.py:18
  446.3 16.3 %collective-permute-start.31 = (f32[1,2,1024]{2,1,0:T(2,128)}, f32[1,2,1024]{2,1,0:T(2,128)}, u32[]{:S(2)}, u32[]{:S(2)}) collective-permute-start(f32[1,2,1024]{2,1,0:T(2,128)} %stack_reshape_squeeze.42), channel_id=1, source_target_pairs={{1,0},{2,1},{3,2},{4,3},{5,4},{6,5},{7,6},{8,7},{9,8},{10,9},{11,1... | collective-permute-start | bytes 24584 | tf_op jit(solution)/shard_map/ppermute | solution.py:21
  477.2 5.1 collective-permute-start.35
  482.3 4.2 collective-permute-start.36
  486.5 5.7 collective-permute-start.37
  492.2 7.1 collective-permute-start.38
  499.9 12.6 %collective-permute-start.39 = (f32[257]{0:T(512)}, f32[257]{0:T(512)}, u32[]{:S(2)}, u32[]{:S(2)}) collective-permute-start(f32[257]{0:T(512)} %add.733), channel_id=1, source_target_pairs={{0,8},{1,9},{2,10},{3,11},{4,12},{5,13},{6,14},{7,15},{8,0},{9,1},... | collective-permute-start | bytes 3092 | tf_op jit(solution)/shard_map/ppermute | solution.py:198
  551.6 25.7 %collective-permute-start.41 = (f32[1,2,1024]{2,1,0:T(2,128)}, f32[1,2,1024]{2,1,0:T(2,128)}, u32[]{:S(2)}, u32[]{:S(2)}) collective-permute-start(f32[1,2,1024]{2,1,0:T(2,128)} %stack_reshape_squeeze.45), channel_id=1, source_target_pairs={{0,1},{1,2},{2,3},{3,4},{4,5},{5,6},{6,7},{7,8},{8,9},{9,10},{10,1... | collective-permute-start | bytes 24584 | tf_op jit(solution)/shard_map/ppermute | solution.py:18
  554.1 29.1 %collective-permute-start.40 = (f32[1,2,1024]{2,1,0:T(2,128)}, f32[1,2,1024]{2,1,0:T(2,128)}, u32[]{:S(2)}, u32[]{:S(2)}) collective-permute-start(f32[1,2,1024]{2,1,0:T(2,128)} %stack_reshape_squeeze.44), channel_id=1, source_target_pairs={{1,0},{2,1},{3,2},{4,3},{5,4},{6,5},{7,6},{8,7},{9,8},{10,9},{11,1... | collective-permute-start | bytes 24584 | tf_op jit(solution)/shard_map/ppermute | solution.py:21
  592.9 4.6 collective-permute-start.42
  598.7 3.7 collective-permute-start.43
  603.1 5.2 collective-permute-start.44
  608.9 4.3 collective-permute-start.45
  613.9 5.2 collective-permute-start.46
  619.7 5.3 collective-permute-start.47
  625.6 5.2 collective-permute-start.48
  672.8 12.3 %collective-permute-start.50 = (f32[1,2,1024]{2,1,0:T(2,128)S(1)}, f32[1,2,1024]{2,1,0:T(2,128)S(1)}, u32[]{:S(2)}, u32[]{:S(2)}) collective-permute-start(f32[1,2,1024]{2,1,0:T(2,128)S(1)} %stack_reshape_squeeze.47), channel_id=1, source_target_pairs={{0,1},{1,2},{2,3},{3,4},{4,5},{5,6},{6,7},{7,8},{8,9},{9,10},{10,1... | collective-permute-start | bytes 24584 | tf_op jit(solution)/shard_map/ppermute | solution.py:18
  675.2 14.0 %collective-permute-start.49 = (f32[1,2,1024]{2,1,0:T(2,128)}, f32[1,2,1024]{2,1,0:T(2,128)}, u32[]{:S(2)}, u32[]{:S(2)}) collective-permute-start(f32[1,2,1024]{2,1,0:T(2,128)} %stack_reshape_squeeze.46), channel_id=1, source_target_pairs={{1,0},{2,1},{3,2},{4,3},{5,4},{6,5},{7,6},{8,7},{9,8},{10,9},{11,1... | collective-permute-start | bytes 24584 | tf_op jit(solution)/shard_map/ppermute | solution.py:21
  704.2 5.1 collective-permute-start.53
  709.3 4.2 collective-permute-start.54
  713.5 23.9 %collective-permute-start.55 = (f32[257]{0:T(512)S(1)}, f32[257]{0:T(512)S(1)}, u32[]{:S(2)}, u32[]{:S(2)}) collective-permute-start(f32[257]{0:T(512)S(1)} %add.759), channel_id=1, source_target_pairs={{0,2},{1,3},{2,0},{3,1},{4,6},{5,7},{6,4},{7,5},{8,10},{9,11},{10,... | collective-permute-start | bytes 3092 | tf_op jit(solution)/shard_map/ppermute | solution.py:198
  738.0 12.3 %collective-permute-start.56 = (f32[257]{0:T(512)}, f32[257]{0:T(512)}, u32[]{:S(2)}, u32[]{:S(2)}) collective-permute-start(f32[257]{0:T(512)} %add.760), channel_id=1, source_target_pairs={{0,4},{1,5},{2,6},{3,7},{4,0},{5,1},{6,2},{7,3},{8,12},{9,13},{10,... | collective-permute-start | bytes 3092 | tf_op jit(solution)/shard_map/ppermute | solution.py:198
  751.7 35.1 %collective-permute-start.57 = (f32[257]{0:T(512)}, f32[257]{0:T(512)}, u32[]{:S(2)}, u32[]{:S(2)}) collective-permute-start(f32[257]{0:T(512)} %add.761), channel_id=1, source_target_pairs={{0,8},{1,9},{2,10},{3,11},{4,12},{5,13},{6,14},{7,15},{8,0},{9,1},... | collective-permute-start | bytes 3092 | tf_op jit(solution)/shard_map/ppermute | solution.py:198
  (237 other events, 1978.6 us)
where the time goes:
time: 810 us; the launch traced here: 796 us
  local copies, waits for them, and re-layouts  344 us (42%)
  other arithmetic  145 us (18%)
  starting transfers between devices  145 us (18%)
  blocking collectives  78.8 us (10%)
  waiting for transfers between devices  54 us (7%)
  between operations  25.7 us (3%)
    ppermute x46, starting transfers between devices, butterfly(): values = values + lax.ppermute(values, axis, pairs)  124 us
    all_gather x6, blocking collectives, apply_operator(): portion = lax.all_gather(outgoing_sides[None], 'brick', axis=0, tiled=True)  78.8 us
    ppermute x46, waiting for transfers between devices, butterfly(): values = values + lax.ppermute(values, axis, pairs)  54 us
    broadcast_in_dim x26, local copies, waits for them, and re-layouts, apply_operator(): jnp.where(cube_third == BS - 1, from_above, jnp.roll(cube, -1, axis=3))  46.7 us
    broadcast_in_dim x26, local copies, waits for them, and re-layouts, apply_operator(): jnp.where(cube_third == 0, from_below, jnp.roll(cube, 1, axis=3))  42.9 us
    concatenate x12, local copies, waits for them, and re-layouts, apply_operator(): jnp.roll(cube, 1, axis=3)  25.5 us
    concatenate x12, local copies, waits for them, and re-layouts, apply_operator(): jnp.roll(cube, -1, axis=3)  23 us
    concatenate x15, local copies, waits for them, and re-layouts, apply_operator(): jnp.concatenate([field[:, :, BS:], beyond_yplus], axis=2)  21.9 us
  transfers between devices with their start and end apart: 58, of which 34 were waited for; matrix products, arithmetic and copies ran while one was open for 30% of the time, Pallas kernels for 0%

commit v1 on v0

--- a/solution.py
+++ b/solution.py
@@ -1,3 +1,4 @@
+import functools
 import jax
 import jax.numpy as jnp
 from jax import lax
@@ -8,6 +9,23 @@
 PATCH_Y = 2
 ITERS = 3
 OMEGA = 0.6
+
+
+def name_the_panels(here_x, join_dim):
+    slots = jax.lax.psum(1, axis_name="brick")
+    w_next = range(here_x.ndim)
+    stack_in = list(map(lambda u: slots if u == join_dim else 1, w_next))
+    built = jax.lax.all_to_all(
+        jnp.tile(here_x, stack_in),
+        axis_name="brick",
+        split_axis=join_dim,
+        concat_axis=join_dim,
+        tiled=True,
+    )
+    return built
+
+
+change_masks = functools.partial(name_the_panels, join_dim=0)
 
 
 def extended_2(block, sides, width):
@@ -119,7 +137,7 @@
                 pad_rows(grid_upper_y[:, PATCH_Y - 1], capacity),
             ]
         )
-        portion = lax.all_gather(outgoing_sides[None], "brick", axis=0, tiled=True)
+        portion = change_masks(outgoing_sides[None])
         sources = jnp.arange(portion.shape[0], dtype=jnp.int32)
         matches = sources[:, None] == wanted[None, :]
         remote = jnp.zeros((4, capacity, face_size), jnp.float32) + jnp.sum(

time: 810 us -> 758 us (0.936)
  blocking collectives: 78.8 us -> 0 us
  starting transfers between devices: 145 us -> 188 us
  local copies, waits for them, and re-layouts: 344 us -> 329 us
  waiting for transfers between devices: 54 us -> 42.6 us
  other arithmetic: 145 us -> 154 us
    all_gather x6 -> x0, blocking collectives: 78.8 us -> none  [apply_operator(): portion = lax.all_gather(outgoing_sides[None], 'brick', axis=0, tiled=True)]
    all_to_all x0 -> x6, starting transfers between devices: none -> 28.6 us  [name_the_panels(): jax.lax.all_to_all(jnp.tile(here_x, stack_in), axis_name='brick', split_a...]
    ppermute x46, starting transfers between devices: 124 us -> 139 us  [butterfly(): values = values + lax.ppermute(values, axis, pairs)]
    ppermute x46, waiting for transfers between devices: 54 us -> 42.6 us  [butterfly(): values = values + lax.ppermute(values, axis, pairs)]
    another operation x0 -> x19, local copies, waits for them, and re-layouts: none -> 11.4 us  [the longest x6 4.7 us: name_the_panels(): jnp.tile(here_x, stack_in)]
    concatenate x14 -> x24, local copies, waits for them, and re-layouts: 20.6 us -> 25.5 us  [apply_operator(): jnp.concatenate([field[:, 1:, :], beyond_xplus[:, None, :]], axis=1)]
    concatenate x11 -> x18, local copies, waits for them, and re-layouts: 18.3 us -> 21.5 us  [apply_operator(): jnp.concatenate([beyond_xminus[:, None, :], field[:, :-1, :]], axis=1)]
  transfers between devices with their start and end apart: 58 -> 64, of which waited for: 34 -> 34; matrix products, arithmetic and copies ran while one was open for 30% -> 37% of each run, Pallas kernels for 0% -> 0%
where the time goes in v1:
time: 758 us; the launch traced here: 743 us
  local copies, waits for them, and re-layouts  329 us (43%)
  starting transfers between devices  188 us (25%)
  other arithmetic  154 us (20%)
  waiting for transfers between devices  42.6 us (6%)
  between operations  26.1 us (3%)
    ppermute x46, starting transfers between devices, butterfly(): values = values + lax.ppermute(values, axis, pairs)  139 us
    ppermute x46, waiting for transfers between devices, butterfly(): values = values + lax.ppermute(values, axis, pairs)  42.6 us
    broadcast_in_dim x26, local copies, waits for them, and re-layouts, apply_operator(): jnp.where(cube_third == BS - 1, from_above, jnp.roll(cube, -1, axis=3))  41.1 us
    broadcast_in_dim x26, local copies, waits for them, and re-layouts, apply_operator(): jnp.where(cube_third == 0, from_below, jnp.roll(cube, 1, axis=3))  40.3 us
    all_to_all x6, starting transfers between devices, name_the_panels(): jax.lax.all_to_all(jnp.tile(here_x, stack_in), axis_name='brick', split_a...  28.6 us
    concatenate x24, local copies, waits for them, and re-layouts, apply_operator(): jnp.concatenate([field[:, 1:, :], beyond_xplus[:, None, :]], axis=1)  25.5 us
    concatenate x12, local copies, waits for them, and re-layouts, apply_operator(): jnp.roll(cube, -1, axis=3)  24.2 us
    concatenate x12, local copies, waits for them, and re-layouts, apply_operator(): jnp.roll(cube, 1, axis=3)  24.2 us
  transfers between devices with their start and end apart: 64, of which 34 were waited for; matrix products, arithmetic and copies ran while one was open for 37% of the time, Pallas kernels for 0%

profile of v1, /device:TPU:0, one launch (start us, length us, event | category | flops | bytes accessed | tf_op | source)
XLA Modules:
  0.0 743.1 jit_solution(3704224139463503153)
XLA Ops:
  10.9 4.6 all-to-all-start
  42.1 5.5 multiply_divide_fusion.2
  71.6 5.6 collective-permute-start.3
  80.0 3.6 collective-permute-start.4
  85.6 3.7 collective-permute-start.5
  119.4 8.4 %fusion.46 = (f32[2,32,32,32]{3,2,1,0:T(8,128)S(1)}, f32[2,32,32,32]{3,2,1,0:T(8,128)}, f32[2,32,32,32]{3,2,1,0:T(8,128)}) fusion(f32[2,32,32,32]{3,2,1,0:T(8,128)} %get-tuple-element.67, f32[2,32,32,32]{3,2,1,0:T(8,128)} %copy-done.17, f32[2,32,32,32]{3,2,1,0:T(8,128)} %copy-done.16, f32[2,32,32,32]{3,2,1,0:T(8,128)} %concatenate.668, ...), kind=kLoop, calls=%fused_computation.88 | loop fusion | flops 2293760 | bytes 4538480 | tf_op jit(solution)/shard_map/add | solution.py:249
  150.2 4.8 all-to-all-start.1
  191.2 3.8 multiply_reduce_fusion.4
  204.8 3.4 collective-permute-start.17
  213.9 3.5 collective-permute-start.19
  219.6 4.7 collective-permute-start.20
  240.4 3.4 collective-permute-start.7
  244.7 4.9 collective-permute-start.8
  256.3 3.8 collective-permute-done.10
  265.1 3.2 collective-permute-start.12
  279.0 6.6 multiply_divide_fusion.1
  300.3 4.8 all-to-all-start.2
  349.6 3.7 multiply_reduce_fusion.3
  359.5 3.2 collective-permute-start.25
  363.8 4.7 collective-permute-start.26
  369.7 3.8 collective-permute-start.27
  374.5 3.4 collective-permute-start.28
  380.3 5.2 collective-permute-start.29
  386.5 4.7 collective-permute-start.30
  396.1 6.4 multiply_add_fusion.1
  408.0 4.8 all-to-all-start.3
  435.5 3.4 multiply_reduce_fusion.2
  445.2 3.5 collective-permute-start.35
  454.5 3.9 collective-permute-start.37
  460.0 5.5 collective-permute-start.38
  467.7 3.4 collective-permute-start.39
  486.7 6.2 multiply_divide_fusion
  504.2 4.8 all-to-all-start.4
  514.5 3.1 pad_maximum_fusion.8
  551.7 3.9 multiply_reduce_fusion.1
  561.7 3.2 collective-permute-start.43
  565.9 4.7 collective-permute-start.44
  571.6 3.8 collective-permute-start.45
  576.2 3.7 collective-permute-start.46
  581.9 5.9 collective-permute-start.47
  588.6 4.4 collective-permute-start.48
  598.3 9.3 %multiply_add_fusion = f32[2,32,32,32]{3,2,1,0:T(8,128)S(1)} fusion(f32[2,32,32,32]{3,2,1,0:T(8,128)} %copy-done.18, f32[2,32,32,32]{3,2,1,0:T(8,128)} %get-tuple-element.67, f32[2,32,32,32]{3,2,1,0:T(8,128)} %copy-done.17, f32[2,32,32,32]{3,2,1,0:T(8,128)} %copy-done.16, f32[2,32,32,32]{3,2,1,0:T(8,128)} %concatenate.784, ...), kind=kLoop, calls=%fused_computation.76 | loop fusion | flops 3735552 | bytes 5865592 | tf_op jit(solution)/shard_map/add | solution.py:281
  613.4 4.8 all-to-all-start.5
  649.4 3.5 collective-permute-start.53
  677.2 4.2 collective-permute-start.55
  681.5 3.9 fusion.96
  710.7 3.2 collective-permute-start.57
  736.2 5.8 fusion.148
  (958 shorter events, 500.9 us)
Async XLA Ops:
  10.9 99.4 %all-to-all-start = ((f32[8,4,2,1024]{3,2,1,0:T(2,128)}), f32[8,4,2,1024]{3,2,1,0:T(2,128)}, u32[]{:S(2)}, u32[]{:S(2)}) async-start(f32[8,4,2,1024]{3,2,1,0:T(2,128)} %tile.12), calls=%async_computation | async-start | bytes 524288 | tf_op jit(solution)/shard_map/all_to_all | solution.py:18
  51.3 19.4 %collective-permute-start.2 = (f32[16,5,2]{2,0,1:T(8,128)}, f32[16,5,2]{2,0,1:T(8,128)}, u32[]{:S(2)}, u32[]{:S(2)}) collective-permute-start(f32[16,5,2]{2,0,1:T(8,128)} %broadcast_multiply_fusion.3), channel_id=1, source_target_pairs={{0,1},{1,0},{2,3},{3,2},{4,5},{5,4},{6,7},{7,6},{8,9},{9,8},{10,11... | collective-permute-start | bytes 1928 | tf_op jit(solution)/shard_map/ppermute | solution.py:216
  57.0 47.3 %collective-permute-start.1 = (f32[1,2,1024]{2,1,0:T(2,128)}, f32[1,2,1024]{2,1,0:T(2,128)}, u32[]{:S(2)}, u32[]{:S(2)}) collective-permute-start(f32[1,2,1024]{2,1,0:T(2,128)} %stack_reshape_squeeze.37), channel_id=1, source_target_pairs={{0,1},{1,2},{2,3},{3,4},{4,5},{5,6},{6,7},{7,8},{8,9},{9,10},{10,1... | collective-permute-start | bytes 24584 | tf_op jit(solution)/shard_map/ppermute | solution.py:36
  61.0 40.7 %collective-permute-start = (f32[1,2,1024]{2,1,0:T(2,128)}, f32[1,2,1024]{2,1,0:T(2,128)}, u32[]{:S(2)}, u32[]{:S(2)}) collective-permute-start(f32[1,2,1024]{2,1,0:T(2,128)} %stack_reshape_squeeze.36), channel_id=1, source_target_pairs={{1,0},{2,1},{3,2},{4,3},{5,4},{6,5},{7,6},{8,7},{9,8},{10,9},{11,1... | collective-permute-start | bytes 24584 | tf_op jit(solution)/shard_map/ppermute | solution.py:39
  71.6 7.5 %collective-permute-start.3 = (f32[16,5,2]{2,0,1:T(8,128)S(1)}, f32[16,5,2]{2,0,1:T(8,128)S(1)}, u32[]{:S(2)}, u32[]{:S(2)}) collective-permute-start(f32[16,5,2]{2,0,1:T(8,128)S(1)} %fusion.171), channel_id=1, source_target_pairs={{0,2},{1,3},{2,0},{3,1},{4,6},{5,7},{6,4},{7,5},{8,10},{9,11},{10,... | collective-permute-start | bytes 1928 | tf_op jit(solution)/shard_map/ppermute | solution.py:216
  80.0 5.6 collective-permute-start.4
  85.6 7.6 %collective-permute-start.5 = (f32[16,5,2]{2,0,1:T(8,128)S(1)}, f32[16,5,2]{2,0,1:T(8,128)S(1)}, u32[]{:S(2)}, u32[]{:S(2)}) collective-permute-start(f32[16,5,2]{2,0,1:T(8,128)S(1)} %add.671), channel_id=1, source_target_pairs={{0,8},{1,9},{2,10},{3,11},{4,12},{5,13},{6,14},{7,15},{8,0},{9,1},... | collective-permute-start | bytes 1928 | tf_op jit(solution)/shard_map/ppermute | solution.py:216
  150.2 32.0 %all-to-all-start.1 = ((f32[8,4,2,1024]{3,2,1,0:T(2,128)}), f32[8,4,2,1024]{3,2,1,0:T(2,128)}, u32[]{:S(2)}, u32[]{:S(2)}) async-start(f32[8,4,2,1024]{3,2,1,0:T(2,128)} %tile.13), calls=%async_computation.1 | async-start | bytes 524288 | tf_op jit(solution)/shard_map/all_to_all | solution.py:18
  157.9 12.6 %collective-permute-start.14 = (f32[1,2,1024]{2,1,0:T(2,128)}, f32[1,2,1024]{2,1,0:T(2,128)}, u32[]{:S(2)}, u32[]{:S(2)}) collective-permute-start(f32[1,2,1024]{2,1,0:T(2,128)} %stack_reshape_squeeze.39), channel_id=1, source_target_pairs={{0,1},{1,2},{2,3},{3,4},{4,5},{5,6},{6,7},{7,8},{8,9},{9,10},{10,1... | collective-permute-start | bytes 24584 | tf_op jit(solution)/shard_map/ppermute | solution.py:36
  159.8 16.6 %collective-permute-start.13 = (f32[1,2,1024]{2,1,0:T(2,128)}, f32[1,2,1024]{2,1,0:T(2,128)}, u32[]{:S(2)}, u32[]{:S(2)}) collective-permute-start(f32[1,2,1024]{2,1,0:T(2,128)} %stack_reshape_squeeze.38), channel_id=1, source_target_pairs={{1,0},{2,1},{3,2},{4,3},{5,4},{6,5},{7,6},{8,7},{9,8},{10,9},{11,1... | collective-permute-start | bytes 24584 | tf_op jit(solution)/shard_map/ppermute | solution.py:39
  204.8 5.1 collective-permute-start.17
  213.9 5.1 collective-permute-start.19
  219.6 16.6 %collective-permute-start.20 = (f32[257]{0:T(512)}, f32[257]{0:T(512)}, u32[]{:S(2)}, u32[]{:S(2)}) collective-permute-start(f32[257]{0:T(512)} %add.700), channel_id=1, source_target_pairs={{0,4},{1,5},{2,6},{3,7},{4,0},{5,1},{6,2},{7,3},{8,12},{9,13},{10,... | collective-permute-start | bytes 3092 | tf_op jit(solution)/shard_map/ppermute | solution.py:216
  231.6 7.5 %collective-permute-start.6 = (f32[1]{0:T(128)}, f32[1]{0:T(128)}, u32[]{:S(2)}, u32[]{:S(2)}) collective-permute-start(f32[1]{0:T(128)} %bitcast.39), channel_id=1, source_target_pairs={{0,16},{16,0},{32,48},{48,32},{64,80},{80,64},{96,112},{112,96},{1... | collective-permute-start | bytes 20 | tf_op jit(solution)/shard_map/ppermute | solution.py:216
  237.0 34.4 %collective-permute-start.21 = (f32[257]{0:T(512)S(1)}, f32[257]{0:T(512)S(1)}, u32[]{:S(2)}, u32[]{:S(2)}) collective-permute-start(f32[257]{0:T(512)S(1)} %add.701), channel_id=1, source_target_pairs={{0,8},{1,9},{2,10},{3,11},{4,12},{5,13},{6,14},{7,15},{8,0},{9,1},... | collective-permute-start | bytes 3092 | tf_op jit(solution)/shard_map/ppermute | solution.py:216
  244.7 5.2 collective-permute-start.8
  254.9 5.2 collective-permute-start.10
  265.1 5.6 collective-permute-start.12
  300.3 37.6 %all-to-all-start.2 = ((f32[8,4,2,1024]{3,2,1,0:T(2,128)}), f32[8,4,2,1024]{3,2,1,0:T(2,128)}, u32[]{:S(2)}, u32[]{:S(2)}) async-start(f32[8,4,2,1024]{3,2,1,0:T(2,128)} %tile.14), calls=%async_computation.2 | async-start | bytes 524288 | tf_op jit(solution)/shard_map/all_to_all | solution.py:18
  308.0 18.2 %collective-permute-start.23 = (f32[1,2,1024]{2,1,0:T(2,128)}, f32[1,2,1024]{2,1,0:T(2,128)}, u32[]{:S(2)}, u32[]{:S(2)}) collective-permute-start(f32[1,2,1024]{2,1,0:T(2,128)} %stack_reshape_squeeze.41), channel_id=1, source_target_pairs={{0,1},{1,2},{2,3},{3,4},{4,5},{5,6},{6,7},{7,8},{8,9},{9,10},{10,1... | collective-permute-start | bytes 24584 | tf_op jit(solution)/shard_map/ppermute | solution.py:36
  310.5 21.5 %collective-permute-start.22 = (f32[1,2,1024]{2,1,0:T(2,128)}, f32[1,2,1024]{2,1,0:T(2,128)}, u32[]{:S(2)}, u32[]{:S(2)}) collective-permute-start(f32[1,2,1024]{2,1,0:T(2,128)} %stack_reshape_squeeze.40), channel_id=1, source_target_pairs={{1,0},{2,1},{3,2},{4,3},{5,4},{6,5},{7,6},{8,7},{9,8},{10,9},{11,1... | collective-permute-start | bytes 24584 | tf_op jit(solution)/shard_map/ppermute | solution.py:39
  353.3 4.9 collective-permute-start.24
  363.8 5.2 collective-permute-start.26
  374.5 5.2 collective-permute-start.28
  380.3 5.5 collective-permute-start.29
  386.5 5.4 collective-permute-start.30
  408.0 24.3 %all-to-all-start.3 = ((f32[8,4,2,1024]{3,2,1,0:T(2,128)}), f32[8,4,2,1024]{3,2,1,0:T(2,128)}, u32[]{:S(2)}, u32[]{:S(2)}) async-start(f32[8,4,2,1024]{3,2,1,0:T(2,128)} %tile.15), calls=%async_computation.3 | async-start | bytes 524288 | tf_op jit(solution)/shard_map/all_to_all | solution.py:18
  413.6 11.2 %collective-permute-start.32 = (f32[1,2,1024]{2,1,0:T(2,128)S(1)}, f32[1,2,1024]{2,1,0:T(2,128)S(1)}, u32[]{:S(2)}, u32[]{:S(2)}) collective-permute-start(f32[1,2,1024]{2,1,0:T(2,128)S(1)} %stack_reshape_squeeze.43), channel_id=1, source_target_pairs={{0,1},{1,2},{2,3},{3,4},{4,5},{5,6},{6,7},{7,8},{8,9},{9,10},{10,1... | collective-permute-start | bytes 24584 | tf_op jit(solution)/shard_map/ppermute | solution.py:36
  415.8 12.0 %collective-permute-start.31 = (f32[1,2,1024]{2,1,0:T(2,128)}, f32[1,2,1024]{2,1,0:T(2,128)}, u32[]{:S(2)}, u32[]{:S(2)}) collective-permute-start(f32[1,2,1024]{2,1,0:T(2,128)} %stack_reshape_squeeze.42), channel_id=1, source_target_pairs={{1,0},{2,1},{3,2},{4,3},{5,4},{6,5},{7,6},{8,7},{9,8},{10,9},{11,1... | collective-permute-start | bytes 24584 | tf_op jit(solution)/shard_map/ppermute | solution.py:39
  445.2 5.1 collective-permute-start.35
  454.5 5.4 collective-permute-start.37
  460.0 7.1 collective-permute-start.38
  467.7 12.5 %collective-permute-start.39 = (f32[257]{0:T(512)}, f32[257]{0:T(512)}, u32[]{:S(2)}, u32[]{:S(2)}) collective-permute-start(f32[257]{0:T(512)} %add.733), channel_id=1, source_target_pairs={{0,8},{1,9},{2,10},{3,11},{4,12},{5,13},{6,14},{7,15},{8,0},{9,1},... | collective-permute-start | bytes 3092 | tf_op jit(solution)/shard_map/ppermute | solution.py:216
  504.2 35.7 %all-to-all-start.4 = ((f32[8,4,2,1024]{3,2,1,0:T(2,128)}), f32[8,4,2,1024]{3,2,1,0:T(2,128)}, u32[]{:S(2)}, u32[]{:S(2)}) async-start(f32[8,4,2,1024]{3,2,1,0:T(2,128)} %tile.16), calls=%async_computation.4 | async-start | bytes 524288 | tf_op jit(solution)/shard_map/all_to_all | solution.py:18
  511.3 17.6 %collective-permute-start.41 = (f32[1,2,1024]{2,1,0:T(2,128)S(1)}, f32[1,2,1024]{2,1,0:T(2,128)S(1)}, u32[]{:S(2)}, u32[]{:S(2)}) collective-permute-start(f32[1,2,1024]{2,1,0:T(2,128)S(1)} %stack_reshape_squeeze.45), channel_id=1, source_target_pairs={{0,1},{1,2},{2,3},{3,4},{4,5},{5,6},{6,7},{7,8},{8,9},{9,10},{10,1... | collective-permute-start | bytes 24584 | tf_op jit(solution)/shard_map/ppermute | solution.py:36
  513.2 20.9 %collective-permute-start.40 = (f32[1,2,1024]{2,1,0:T(2,128)}, f32[1,2,1024]{2,1,0:T(2,128)}, u32[]{:S(2)}, u32[]{:S(2)}) collective-permute-start(f32[1,2,1024]{2,1,0:T(2,128)} %stack_reshape_squeeze.44), channel_id=1, source_target_pairs={{1,0},{2,1},{3,2},{4,3},{5,4},{6,5},{7,6},{8,7},{9,8},{10,9},{11,1... | collective-permute-start | bytes 24584 | tf_op jit(solution)/shard_map/ppermute | solution.py:39
  565.9 5.1 collective-permute-start.44
  576.2 5.1 collective-permute-start.46
  581.9 6.1 collective-permute-start.47
  588.6 5.1 collective-permute-start.48
  613.4 21.8 %all-to-all-start.5 = ((f32[8,4,2,1024]{3,2,1,0:T(2,128)}), f32[8,4,2,1024]{3,2,1,0:T(2,128)}, u32[]{:S(2)}, u32[]{:S(2)}) async-start(f32[8,4,2,1024]{3,2,1,0:T(2,128)} %tile.17), calls=%async_computation.5 | async-start | bytes 524288 | tf_op jit(solution)/shard_map/all_to_all | solution.py:18
  618.4 10.3 %collective-permute-start.50 = (f32[1,2,1024]{2,1,0:T(2,128)S(1)}, f32[1,2,1024]{2,1,0:T(2,128)S(1)}, u32[]{:S(2)}, u32[]{:S(2)}) collective-permute-start(f32[1,2,1024]{2,1,0:T(2,128)S(1)} %stack_reshape_squeeze.47), channel_id=1, source_target_pairs={{0,1},{1,2},{2,3},{3,4},{4,5},{5,6},{6,7},{7,8},{8,9},{9,10},{10,1... | collective-permute-start | bytes 24584 | tf_op jit(solution)/shard_map/ppermute | solution.py:36
  620.3 11.1 %collective-permute-start.49 = (f32[1,2,1024]{2,1,0:T(2,128)S(1)}, f32[1,2,1024]{2,1,0:T(2,128)S(1)}, u32[]{:S(2)}, u32[]{:S(2)}) collective-permute-start(f32[1,2,1024]{2,1,0:T(2,128)S(1)} %stack_reshape_squeeze.46), channel_id=1, source_target_pairs={{1,0},{2,1},{3,2},{4,3},{5,4},{6,5},{7,6},{8,7},{9,8},{10,9},{11,1... | collective-permute-start | bytes 24584 | tf_op jit(solution)/shard_map/ppermute | solution.py:39
  649.4 5.1 collective-permute-start.53
  654.5 22.7 %collective-permute-start.54 = (f32[257]{0:T(512)S(1)}, f32[257]{0:T(512)S(1)}, u32[]{:S(2)}, u32[]{:S(2)}) collective-permute-start(f32[257]{0:T(512)S(1)} %add.758), channel_id=1, source_target_pairs={{0,1},{1,0},{2,3},{3,2},{4,5},{5,4},{6,7},{7,6},{8,9},{9,8},{10,11... | collective-permute-start | bytes 3092 | tf_op jit(solution)/shard_map/ppermute | solution.py:216
  677.2 8.1 %collective-permute-start.55 = (f32[257]{0:T(512)S(1)}, f32[257]{0:T(512)S(1)}, u32[]{:S(2)}, u32[]{:S(2)}) collective-permute-start(f32[257]{0:T(512)S(1)} %add.759), channel_id=1, source_target_pairs={{0,2},{1,3},{2,0},{3,1},{4,6},{5,7},{6,4},{7,5},{8,10},{9,11},{10,... | collective-permute-start | bytes 3092 | tf_op jit(solution)/shard_map/ppermute | solution.py:216
  685.9 23.5 %collective-permute-start.56 = (f32[257]{0:T(512)}, f32[257]{0:T(512)}, u32[]{:S(2)}, u32[]{:S(2)}) collective-permute-start(f32[257]{0:T(512)} %add.760), channel_id=1, source_target_pairs={{0,4},{1,5},{2,6},{3,7},{4,0},{5,1},{6,2},{7,3},{8,12},{9,13},{10,... | collective-permute-start | bytes 3092 | tf_op jit(solution)/shard_map/ppermute | solution.py:216
  710.7 23.5 %collective-permute-start.57 = (f32[257]{0:T(512)}, f32[257]{0:T(512)}, u32[]{:S(2)}, u32[]{:S(2)}) collective-permute-start(f32[257]{0:T(512)} %add.761), channel_id=1, source_target_pairs={{0,8},{1,9},{2,10},{3,11},{4,12},{5,13},{6,14},{7,15},{8,0},{9,1},... | collective-permute-start | bytes 3092 | tf_op jit(solution)/shard_map/ppermute | solution.py:216
  (233 other events, 1776.3 us)
